TPU v7x, 32 devices: a whole 2x2x4 slice. The times are simulated.
32 devices in a mesh: dp: 8 (over z, x), tensor: 4 (over y, core).
Axes of the slice: x: 2, y: 2, z: 4, core: 2. Of those that a mesh axis runs over, the one named last changes fastest.
Arguments:
- tokens: bfloat16 [32768, 768], P(('dp', 'tensor')), may hold values from -6 to 6
- cotangent: bfloat16 [32768, 768], P(('dp', 'tensor')), may hold values from -26 to 26
- seq_group: int32 [16], P('dp'), may hold values from 0 to 1
- block_slot: int32 [13830], replicated, may hold values from 0 to 20751, as said below
- master: float32 [4, 20752, 128], P('tensor', 'dp'), may hold values from -3 to 3
- first_moment: float32 [4, 20752, 128], P('tensor', 'dp'), may hold values from -1 to 1
- second_moment: float32 [4, 20752, 128], P('tensor', 'dp'), may hold values from 0 to 1, as said below
Outputs:
- output: bfloat16 [32768, 768], P(('dp', 'tensor'))
- input_grad: float32 [32768, 768], P(('dp', 'tensor'))
- group_norms: float32 [16], P('dp')
- new_master: float32 [4, 20752, 128], P('tensor', 'dp')
- new_first: float32 [4, 20752, 128], P('tensor', 'dp')
- new_second: float32 [4, 20752, 128], P('tensor', 'dp')
Inputs may be any that keep to these rules, and one draw needn't show every extreme that they name: `block_slot`: all entries differ; slot s belongs to the owner with dp index s // 2594; one owner holds 2594 blocks. `seq_group`: group ids count within one dp index: sequences of different dp indices never share a group. `second_moment`: Positive.
All inputs are finite; a program needn't handle non-finite values.
Results may differ from a plain program's by a relative error of at most 0.012.
Values may be sent and summed in bfloat16 or wider, within the bound.
No kernel may reach another device: no remote copies, remote signals or barrier semaphores. Data moves between devices by JAX's collectives and lax.ppermute only.
A program may use at most 256 MiB of HBM per device.

v0:
```python
import jax
import jax.numpy as jnp
from jax import lax
from jax.sharding import PartitionSpec as P

HEADS = 12
HD = 64
ROT = 16
FF = 3072
eps_norm = 1e-05
eps_adam = 1e-08
beta_one = 0.5
beta_two = 0.6
root_half = 0.7071067811865476
inv_root_tau = 0.3989422804014327


def rotary_tables(length, rot_dims):
    half_rot = rot_dims // 2
    frequency = 10000.0 ** (-2.0 * jnp.arange(half_rot, dtype=jnp.float32) / rot_dims)
    angles = jnp.arange(length, dtype=jnp.float32)[:, None] * frequency[None, :]
    return (jnp.cos(angles), jnp.sin(angles))


def rotate(features, cosine, sine_table, rot_dims):
    half_rot = rot_dims // 2
    first_half = features[..., :half_rot]
    second_half = features[..., half_rot:rot_dims]
    cos_cols = cosine[:, None, :]
    sin_cols = sine_table[:, None, :]
    return jnp.concatenate(
        [
            first_half * cos_cols - second_half * sin_cols,
            second_half * cos_cols + first_half * sin_cols,
            features[..., rot_dims:],
        ],
        axis=-1,
    )


def unrotate(grad_in, cosine, sine_table, rot_dims):
    half_rot = rot_dims // 2
    first_half = grad_in[..., :half_rot]
    second_half = grad_in[..., half_rot:rot_dims]
    cos_cols = cosine[:, None, :]
    sin_cols = sine_table[:, None, :]
    return jnp.concatenate(
        [
            first_half * cos_cols + second_half * sin_cols,
            second_half * cos_cols - first_half * sin_cols,
            grad_in[..., rot_dims:],
        ],
        axis=-1,
    )


def layer_norm(rows_in):
    row_mean = jnp.mean(rows_in, axis=-1, keepdims=True)
    centred = rows_in - row_mean
    inverse = lax.rsqrt(jnp.mean(centred * centred, axis=-1, keepdims=True) + eps_norm)
    return (centred * inverse, inverse)


def unpack(flat_params, d_model, heads_local, ff_local, width_local):
    inner_width = heads_local * HD
    end_qkv = d_model * 3 * inner_width
    end_out = end_qkv + inner_width * d_model
    end_up = end_out + d_model * ff_local
    end_down = end_up + ff_local * d_model
    return (
        flat_params[:end_qkv].reshape(d_model, 3 * inner_width),
        flat_params[end_qkv:end_out].reshape(inner_width, d_model),
        flat_params[end_out:end_up].reshape(d_model, ff_local),
        flat_params[end_up:end_down].reshape(ff_local, d_model),
        flat_params[end_down:].reshape(4, width_local),
    )


def step_rates(position, d_model, heads_local, head_dim, ff_local, seq_len, ff_all):
    end_qkv = d_model * 3 * heads_local * head_dim
    end_out = end_qkv + heads_local * head_dim * d_model
    end_up = end_out + d_model * ff_local
    end_down = end_up + ff_local * d_model
    matrix_rate = d_model ** (-0.5)
    learn_rate = jnp.where(
        position < end_qkv,
        matrix_rate,
        jnp.where(
            position < end_out,
            (seq_len / (5.0 * d_model)) ** 0.5,
            jnp.where(
                position < end_up,
                matrix_rate,
                jnp.where(position < end_down, ff_all ** (-0.5), 0.1),
            ),
        ),
    )
    weight_decay = jnp.where(position < end_down, 0.1, 0.0)
    return (learn_rate.astype(jnp.float32), weight_decay.astype(jnp.float32))


def adam_update(weight, moment_one, moment_two, gradient, learn_rate, weight_decay):
    new_one = beta_one * moment_one + (1.0 - beta_one) * gradient
    new_two = beta_two * moment_two + (1.0 - beta_two) * gradient * gradient
    new_weight = weight - learn_rate * (
        new_one / (jnp.sqrt(new_two) + eps_adam) + weight_decay * weight
    )
    return (new_weight, new_one, new_two)


def by_sequence(tensor_in, seq_count):
    return tensor_in.reshape(seq_count, -1, tensor_in.shape[-1])


def seq_product(left, right, seq_count):
    return jnp.einsum(
        "sli,slj->sij",
        by_sequence(left, seq_count),
        by_sequence(right, seq_count),
        preferred_element_type=jnp.float32,
    )


def on_device(tokens, cotangent, seq_group, block_slot, master, first_moment, second_moment):
    tensor_count = lax.axis_size("tensor")
    tensor_rank = lax.axis_index("tensor")
    owner_index = lax.axis_index("dp")
    owner_count = lax.axis_size("dp")
    d_model = tokens.shape[1]
    local_rows = tokens.shape[0]
    width_local = d_model // tensor_count
    heads_local = HEADS // tensor_count
    inner_width = heads_local * HD
    ff_local = FF // tensor_count
    seq_count = seq_group.shape[0]
    tok_count = local_rows * tensor_count
    seq_len = tok_count // seq_count
    capacity = master.shape[1]
    block_width = master.shape[2]
    block_count = block_slot.shape[0]
    copies = lax.all_gather(master[0].astype(jnp.bfloat16), "dp", axis=0, tiled=True)
    flat_params = copies[block_slot].reshape(-1)
    w_qkv, w_out, w_up, w_down, norm_local = unpack(
        flat_params, d_model, heads_local, ff_local, width_local
    )
    x_full, norm_rows = (
        lax.all_gather(tokens, "tensor", axis=0, tiled=True),
        lax.all_gather(norm_local.reshape(1, 4 * width_local), "tensor", axis=0, tiled=True),
    )
    norm_full = jnp.transpose(norm_rows.reshape(tensor_count, 4, width_local), (1, 0, 2)).reshape(
        4, d_model
    )
    rows_full = x_full.astype(jnp.float32)
    normed, inverse = layer_norm(rows_full)
    norm_gains = norm_full.astype(jnp.float32)
    first_in = (normed * norm_gains[0] + norm_gains[1]).astype(jnp.bfloat16)
    second_in = (normed * norm_gains[2] + norm_gains[3]).astype(jnp.bfloat16)
    projected = jnp.dot(first_in, w_qkv, preferred_element_type=jnp.float32).reshape(
        seq_count, seq_len, 3, heads_local, HD
    )
    cosine, sine_table = rotary_tables(seq_len, ROT)
    queries = rotate(projected[:, :, 0], cosine, sine_table, ROT).astype(jnp.bfloat16)
    key_rows = rotate(projected[:, :, 1], cosine, sine_table, ROT).astype(jnp.bfloat16)
    values = projected[:, :, 2].astype(jnp.bfloat16)
    block_rows = min(512, seq_len)
    block_total = seq_len // block_rows
    scale_factor = HD ** (-0.5)
    starts = jnp.arange(block_total, dtype=jnp.int32) * block_rows
    key_index = jnp.arange(seq_len, dtype=jnp.int32)

    def scores_of(row_start):
        query_block = lax.dynamic_slice_in_dim(queries, row_start, block_rows, 1)
        scores = (
            jnp.einsum("sqhd,skhd->shqk", query_block, key_rows, preferred_element_type=jnp.float32)
            * scale_factor
        )
        allowed = (row_start + jnp.arange(block_rows, dtype=jnp.int32))[:, None] >= key_index[
            None, :
        ]
        return (jnp.where(allowed, scores, -1e30), query_block)

    def forward_block(row_start):
        scores = scores_of(row_start)[0]
        row_peak = jnp.max(scores, axis=-1, keepdims=True)
        exp_scores = jnp.exp(scores - row_peak)
        row_total = jnp.sum(exp_scores, axis=-1, keepdims=True)
        weights_low = (exp_scores / row_total).astype(jnp.bfloat16)
        mixed_heads = jnp.einsum(
            "shqk,skhd->sqhd", weights_low, values, preferred_element_type=jnp.float32
        )
        return (mixed_heads, row_peak + jnp.log(row_total))

    mixed_heads, log_sums = lax.map(forward_block, starts)
    attended = jnp.moveaxis(mixed_heads, 0, 1).reshape(tok_count, inner_width).astype(jnp.bfloat16)
    hidden_pre = jnp.dot(second_in, w_up, preferred_element_type=jnp.float32)
    hidden_low = jax.nn.gelu(hidden_pre, approximate=False).astype(jnp.bfloat16)
    branch = jnp.dot(attended, w_out, preferred_element_type=jnp.float32) + jnp.dot(
        hidden_low, w_down, preferred_element_type=jnp.float32
    )
    branch_sum = lax.psum_scatter(
        branch.astype(jnp.bfloat16), "tensor", scatter_dimension=0, tiled=True
    ).astype(jnp.float32)
    output = (tokens.astype(jnp.float32) + branch_sum).astype(jnp.bfloat16)
    back_full = lax.all_gather(cotangent, "tensor", axis=0, tiled=True)
    grad_down = seq_product(hidden_low, back_full, seq_count)
    grad_hidden = jnp.dot(back_full, w_down.T, preferred_element_type=jnp.float32)
    cumulative = 0.5 * (1.0 + lax.erf(hidden_pre * root_half))
    density = jnp.exp(-0.5 * hidden_pre * hidden_pre) * inv_root_tau
    grad_pre = (grad_hidden * (cumulative + hidden_pre * density)).astype(jnp.bfloat16)
    grad_up = seq_product(second_in, grad_pre, seq_count)
    second_back = jnp.dot(grad_pre, w_up.T, preferred_element_type=jnp.float32)
    grad_out = seq_product(attended, back_full, seq_count)
    grad_attended = jnp.dot(back_full, w_out.T, preferred_element_type=jnp.float32).astype(
        jnp.bfloat16
    )
    grad_blocks_in = jnp.moveaxis(
        grad_attended.reshape(seq_count, block_total, block_rows, heads_local, HD), 1, 0
    )

    def backward_block(carried, inputs):
        row_start, log_sum, grad_block = inputs
        scores, query_block = scores_of(row_start)
        probs = jnp.exp(scores - log_sum)
        grad_probs = jnp.einsum(
            "sqhd,skhd->shqk", grad_block, values, preferred_element_type=jnp.float32
        )
        row_dot = jnp.sum(probs * grad_probs, axis=-1, keepdims=True)
        grad_scores = (probs * (grad_probs - row_dot)).astype(jnp.bfloat16)
        grad_query = (
            jnp.einsum("shqk,skhd->sqhd", grad_scores, key_rows, preferred_element_type=jnp.float32)
            * scale_factor
        )
        grad_keys = (
            carried[0]
            + jnp.einsum(
                "shqk,sqhd->skhd", grad_scores, query_block, preferred_element_type=jnp.float32
            )
            * scale_factor
        )
        grad_values = carried[1] + jnp.einsum(
            "shqk,sqhd->skhd",
            probs.astype(jnp.bfloat16),
            grad_block,
            preferred_element_type=jnp.float32,
        )
        return ((grad_keys, grad_values), grad_query)

    zero_heads = jnp.zeros((seq_count, seq_len, heads_local, HD), jnp.float32)
    key_value_grads, grad_queries = lax.scan(
        backward_block, (zero_heads, zero_heads), (starts, log_sums, grad_blocks_in)
    )
    grad_queries = jnp.moveaxis(grad_queries, 0, 1).reshape(seq_count, seq_len, heads_local, HD)
    grad_qkv = (
        jnp.stack(
            [
                unrotate(grad_queries, cosine, sine_table, ROT),
                unrotate(key_value_grads[0], cosine, sine_table, ROT),
                key_value_grads[1],
            ],
            axis=2,
        )
        .reshape(tok_count, 3 * inner_width)
        .astype(jnp.bfloat16)
    )
    grad_qkv_w = seq_product(first_in, grad_qkv, seq_count)
    first_back = jnp.dot(grad_qkv, w_qkv.T, preferred_element_type=jnp.float32)
    row_start_local = tensor_rank * local_rows
    first_sum, second_sum = (
        lax.psum_scatter(
            first_back.astype(jnp.bfloat16), "tensor", scatter_dimension=0, tiled=True
        ).astype(jnp.float32),
        lax.psum_scatter(
            second_back.astype(jnp.bfloat16), "tensor", scatter_dimension=0, tiled=True
        ).astype(jnp.float32),
    )
    normed_rows = lax.dynamic_slice_in_dim(normed, row_start_local, local_rows, 0)
    inverse_rows = lax.dynamic_slice_in_dim(inverse, row_start_local, local_rows, 0)
    scaled_first = first_sum * norm_gains[0]
    scaled_second = second_sum * norm_gains[2]
    first_mean = jnp.mean(scaled_first, axis=1, keepdims=True)
    first_cross = jnp.mean(scaled_first * normed_rows, axis=1, keepdims=True)
    second_mean = jnp.mean(scaled_second, axis=1, keepdims=True)
    second_cross = jnp.mean(scaled_second * normed_rows, axis=1, keepdims=True)
    grad_input = (
        cotangent.astype(jnp.float32)
        + inverse_rows * (scaled_first - first_mean - normed_rows * first_cross)
        + inverse_rows * (scaled_second - second_mean - normed_rows * second_cross)
    )
    row_seq = (row_start_local + jnp.arange(local_rows, dtype=jnp.int32)) // seq_len
    row_member = (row_seq[None, :] == jnp.arange(seq_count, dtype=jnp.int32)[:, None]).astype(
        jnp.float32
    )
    partial_sums = jnp.stack(
        [
            jnp.dot(row_member, first_sum * normed_rows, precision=lax.Precision.HIGHEST),
            jnp.dot(row_member, first_sum, precision=lax.Precision.HIGHEST),
            jnp.dot(row_member, second_sum * normed_rows, precision=lax.Precision.HIGHEST),
            jnp.dot(row_member, second_sum, precision=lax.Precision.HIGHEST),
        ],
        axis=1,
    )
    norm_grads = lax.psum_scatter(partial_sums, "tensor", scatter_dimension=2, tiled=True)
    per_seq = jnp.concatenate(
        [
            grad_qkv_w.reshape(seq_count, -1),
            grad_out.reshape(seq_count, -1),
            grad_up.reshape(seq_count, -1),
            grad_down.reshape(seq_count, -1),
            norm_grads.reshape(seq_count, -1),
        ],
        axis=1,
    )
    member = (seq_group[None, :] == jnp.arange(seq_count, dtype=jnp.int32)[:, None]).astype(
        jnp.float32
    )
    group_grads = jnp.dot(member, per_seq, precision=lax.Precision.HIGHEST)
    squares = lax.psum(jnp.sum(group_grads * group_grads, axis=1), "tensor")
    group_norms = jnp.sqrt(squares)
    clip_scale = 1.0 / jnp.maximum(group_norms, 1.0)
    clipped = jnp.dot(clip_scale, group_grads, precision=lax.Precision.HIGHEST)
    grad_rows = clipped.reshape(block_count, block_width)
    slot_total = owner_count * capacity
    slot_block = (
        jnp.full((slot_total,), -1, jnp.int32)
        .at[block_slot]
        .set(jnp.arange(block_count, dtype=jnp.int32))
    )
    my_blocks = lax.dynamic_slice_in_dim(slot_block, owner_index * capacity, capacity)
    summed = lax.psum(grad_rows, "dp")
    owned_grad = jnp.where(my_blocks[:, None] >= 0, summed[jnp.maximum(my_blocks, 0)], 0.0)
    position = (
        jnp.maximum(my_blocks, 0)[:, None] * block_width
        + jnp.arange(block_width, dtype=jnp.int32)[None, :]
    )
    learn_rate, weight_decay = step_rates(position, d_model, heads_local, HD, ff_local, seq_len, FF)
    new_weight, new_one, new_two = adam_update(
        master[0], first_moment[0], second_moment[0], owned_grad, learn_rate, weight_decay
    )
    return (output, grad_input, group_norms, new_weight[None], new_one[None], new_two[None])


def solution(mesh):
    placed = (
        P(("dp", "tensor"), None),
        P(("dp", "tensor"), None),
        P("dp"),
        P(),
        P("tensor", "dp", None),
        P("tensor", "dp", None),
        P("tensor", "dp", None),
    )
    return jax.shard_map(
        on_device,
        mesh=mesh,
        in_specs=placed,
        out_specs=(
            P(("dp", "tensor"), None),
            P(("dp", "tensor"), None),
            P("dp"),
            P("tensor", "dp", None),
            P("tensor", "dp", None),
            P("tensor", "dp", None),
        ),
        check_vma=False,
    )
```

profile of v0, /device:TPU:0, one launch (start us, length us, event | category | flops | bytes accessed | tf_op | source)
XLA Modules:
  0.0 1451.3 jit_solution(10674566761597092681)
XLA Ops:
  17.1 148.8 %all-gather.10.cloned.1.call-done = bf16[1,20752,128]{2,0,1:T(2,128)(2,1)} async-done(((bf16[1,2594,128]{2,0,1:T(2,128)(2,1)}), bf16[1,20752,128]{2,0,1:T(2,128)(2,1)}) %all-gather.10.cloned.1.call-update) | async-done | bytes 5312528 | tf_op jit(solution)/shard_map/all_gather | solution.py:141
  165.9 8.5 copy.115
  174.4 30.7 %gather_fusion = bf16[13830,128]{1,0:T(8,128)(2,1)S(1)} fusion(bf16[20752,128]{1,0:T(8,128)(2,1)} %bitcast.203, s32[14336]{0:T(1024)} %pad_clamp_fusion), kind=kCustom, calls=%fused_computation | custom fusion | bytes 7136280 | tf_op jit(solution)/shard_map/gather | solution.py:142
  234.9 7.9 fusion.36
  250.1 10.0 all-gather.8.cloned.1.call-done
  260.0 6.1 fusion.55
  276.1 163.2 %while.30 = (s32[]{:T(128)}, bf16[4,2,512,3,64]{2,4,3,1,0:T(8,128)(2,1)}, f32[4,2,3,512,1]{3,2,1,4,0:T(4,128)S(1)}, s32[4]{0:T(128)S(1)}, bf16[2,2048,3,64]{1,3,...) while((s32[]{:T(128)}, ...), condition=%wide.region_5.6_spmd.clone.clone, body=%wide.region_2.5_spmd.clone.sunk.clone | while | flops 1687156224 | bytes 96723152 | solution.py:193
  280.0 12.1 fusion.178
  292.1 12.1 fusion.179
  304.2 11.6 fusion.180
  320.8 12.1 fusion.178
  332.9 12.1 fusion.179
  345.0 11.6 fusion.180
  361.6 12.1 fusion.178
  373.7 12.1 fusion.179
  385.8 11.6 fusion.180
  402.4 12.1 fusion.178
  414.5 12.1 fusion.179
  426.6 11.6 fusion.180
  439.3 336.2 %while.31 = (s32[]{:T(128)}, f32[2,2048,3,64]{1,3,2,0:T(8,128)}, f32[2,2048,3,64]{1,3,2,0:T(8,128)}, f32[4,2,512,3,64]{2,4,3,1,0:T(8,128)}, s32[4]{0:T(128)S(1)}...) while((s32[]{:T(128)}, f32[2,2048,3,64]{1,3,2,0:T(8,128)}, ...), condition=%wide.region_9.10_spmd.clone.clone, body=%wide.region_7.9_spmd.clone.sunk.clone | while | flops 4126078464 | bytes 275603712 | solution.py:249
  443.5 11.3 fusion.190
  454.8 12.9 bitcast_add_fusion.7
  467.7 18.1 %multiply_reduce_fusion.4 = (f32[2,3,512]{2,1,0:T(4,128)S(1)}, f32[2,3,512,2048]{3,2,1,0:T(8,128)}) fusion(f32[2,3,512,2048]{3,2,1,0:T(8,128)} %fusion.190, f32[2,3,512]{2,1,0:T(4,128)S(1)} %dynamic-slice_bitcast_fusion.3, pred[512,2048]{1,0:T(8,128)(4,1)S(1)} %iota_compare_fusion.12, bf16[2,2048,3,64]{1,3,2,0:T(8,128)(2,1)} %copy-done.1, ...), kind=kOutput, calls=%fused_computation.22.clone.1.clone | convolution fusion | flops 836760576 | bytes 53370884 | tf_op jit(solution)/shard_map/while/body/eval_jaxpr/sqhd,skhd->shqk/dot_general | solution.py:224
  485.8 17.0 %multiply_convert_fusion.3 = bf16[2,3,512,2048]{3,2,1,0:T(8,128)(2,1)S(1)} fusion(f32[2,3,512,2048]{3,2,1,0:T(8,128)} %get-tuple-element.409, f32[2,3,512,2048]{3,2,1,0:T(8,128)} %fusion.190, f32[2,3,512]{2,1,0:T(4,128)S(1)} %get-tuple-element.410, f32[2,3,512]{2,1,0:T(4,128)S(1)} %dynamic-slice_bitcast_fusion.3, ...), kind=kLoop, calls=%fused_computation.21.clone.1.clone | loop fusion | flops 37748736 | bytes 63987712 | tf_op jit(solution)/shard_map/while/body/eval_jaxpr/convert_element_type | solution.py:228
  512.5 9.5 fusion.191
  526.0 11.3 fusion.190
  537.3 13.8 bitcast_add_fusion.7
  551.1 18.1 %multiply_reduce_fusion.4 = (f32[2,3,512]{2,1,0:T(4,128)S(1)}, f32[2,3,512,2048]{3,2,1,0:T(8,128)}) fusion(f32[2,3,512,2048]{3,2,1,0:T(8,128)} %fusion.190, f32[2,3,512]{2,1,0:T(4,128)S(1)} %dynamic-slice_bitcast_fusion.3, pred[512,2048]{1,0:T(8,128)(4,1)S(1)} %iota_compare_fusion.12, bf16[2,2048,3,64]{1,3,2,0:T(8,128)(2,1)} %copy-done.1, ...), kind=kOutput, calls=%fused_computation.22.clone.1.clone | convolution fusion | flops 836760576 | bytes 53370884 | tf_op jit(solution)/shard_map/while/body/eval_jaxpr/sqhd,skhd->shqk/dot_general | solution.py:224
  569.2 17.0 %multiply_convert_fusion.3 = bf16[2,3,512,2048]{3,2,1,0:T(8,128)(2,1)S(1)} fusion(f32[2,3,512,2048]{3,2,1,0:T(8,128)} %get-tuple-element.409, f32[2,3,512,2048]{3,2,1,0:T(8,128)} %fusion.190, f32[2,3,512]{2,1,0:T(4,128)S(1)} %get-tuple-element.410, f32[2,3,512]{2,1,0:T(4,128)S(1)} %dynamic-slice_bitcast_fusion.3, ...), kind=kLoop, calls=%fused_computation.21.clone.1.clone | loop fusion | flops 37748736 | bytes 63987712 | tf_op jit(solution)/shard_map/while/body/eval_jaxpr/convert_element_type | solution.py:228
  590.8 6.1 bitcast_add_fusion.6
  596.9 9.5 fusion.191
  610.4 11.3 fusion.190
  621.7 13.8 bitcast_add_fusion.7
  635.5 18.1 %multiply_reduce_fusion.4 = (f32[2,3,512]{2,1,0:T(4,128)S(1)}, f32[2,3,512,2048]{3,2,1,0:T(8,128)}) fusion(f32[2,3,512,2048]{3,2,1,0:T(8,128)} %fusion.190, f32[2,3,512]{2,1,0:T(4,128)S(1)} %dynamic-slice_bitcast_fusion.3, pred[512,2048]{1,0:T(8,128)(4,1)S(1)} %iota_compare_fusion.12, bf16[2,2048,3,64]{1,3,2,0:T(8,128)(2,1)} %copy-done.1, ...), kind=kOutput, calls=%fused_computation.22.clone.1.clone | convolution fusion | flops 836760576 | bytes 53370884 | tf_op jit(solution)/shard_map/while/body/eval_jaxpr/sqhd,skhd->shqk/dot_general | solution.py:224
  653.6 17.0 %multiply_convert_fusion.3 = bf16[2,3,512,2048]{3,2,1,0:T(8,128)(2,1)S(1)} fusion(f32[2,3,512,2048]{3,2,1,0:T(8,128)} %get-tuple-element.409, f32[2,3,512,2048]{3,2,1,0:T(8,128)} %fusion.190, f32[2,3,512]{2,1,0:T(4,128)S(1)} %get-tuple-element.410, f32[2,3,512]{2,1,0:T(4,128)S(1)} %dynamic-slice_bitcast_fusion.3, ...), kind=kLoop, calls=%fused_computation.21.clone.1.clone | loop fusion | flops 37748736 | bytes 63987712 | tf_op jit(solution)/shard_map/while/body/eval_jaxpr/convert_element_type | solution.py:228
  675.2 6.1 bitcast_add_fusion.6
  681.3 9.5 fusion.191
  694.8 11.3 fusion.190
  706.1 13.8 bitcast_add_fusion.7
  719.9 18.1 %multiply_reduce_fusion.4 = (f32[2,3,512]{2,1,0:T(4,128)S(1)}, f32[2,3,512,2048]{3,2,1,0:T(8,128)}) fusion(f32[2,3,512,2048]{3,2,1,0:T(8,128)} %fusion.190, f32[2,3,512]{2,1,0:T(4,128)S(1)} %dynamic-slice_bitcast_fusion.3, pred[512,2048]{1,0:T(8,128)(4,1)S(1)} %iota_compare_fusion.12, bf16[2,2048,3,64]{1,3,2,0:T(8,128)(2,1)} %copy-done.1, ...), kind=kOutput, calls=%fused_computation.22.clone.1.clone | convolution fusion | flops 836760576 | bytes 53370884 | tf_op jit(solution)/shard_map/while/body/eval_jaxpr/sqhd,skhd->shqk/dot_general | solution.py:224
  738.0 17.0 %multiply_convert_fusion.3 = bf16[2,3,512,2048]{3,2,1,0:T(8,128)(2,1)S(1)} fusion(f32[2,3,512,2048]{3,2,1,0:T(8,128)} %get-tuple-element.409, f32[2,3,512,2048]{3,2,1,0:T(8,128)} %fusion.190, f32[2,3,512]{2,1,0:T(4,128)S(1)} %get-tuple-element.410, f32[2,3,512]{2,1,0:T(4,128)S(1)} %dynamic-slice_bitcast_fusion.3, ...), kind=kLoop, calls=%fused_computation.21.clone.1.clone | loop fusion | flops 37748736 | bytes 63987712 | tf_op jit(solution)/shard_map/while/body/eval_jaxpr/convert_element_type | solution.py:228
  765.7 9.5 fusion.191
  788.4 9.5 copy.74
  813.7 9.7 fusion.108
  828.9 9.4 convolution_convert_fusion
  840.7 33.3 %fusion.41 = (bf16[4096,768]{1,0:T(8,128)(2,1)}, f32[4096,768]{1,0:T(8,128)S(1)}) fusion(bf16[4096,768]{1,0:T(8,128)(2,1)} %get-tuple-element.243, bf16[768,768]{1,0:T(8,128)(2,1)S(1)} %copy-done.22), kind=kOutput, calls=%fused_computation.59 | convolution fusion | flops 5036310528 | bytes 26345472 | tf_op jit(solution)/shard_map/dot_general | solution.py:195
  874.0 9.2 fusion.47
  885.8 7.0 convolution_convert_fusion.1
  892.8 9.4 convolution_bitcast_fusion.1
  909.1 6.2 constant_dynamic-update-slice_fusion.2
  917.7 12.2 convolution_bitcast_fusion
  929.9 11.5 fusion.107
  946.8 21.3 %reduce-scatter.11.cloned.1.call-done = bf16[1024,768]{1,0:T(8,128)(2,1)} async-done(((bf16[4096,768]{1,0:T(8,128)(2,1)}), bf16[1024,768]{1,0:T(8,128)(2,1)}) %reduce-scatter.11.cloned.1.call-update) | async-done | bytes 1572880 | tf_op jit(solution)/shard_map/reduce_scatter | solution.py:272
  977.0 9.1 add_convert_fusion
  986.1 8.1 copy.103
  1002.3 41.5 %multiply_reduce_fusion.1 = (f32[2]{0:T(128)S(1)}, f32[2,1770240]{1,0:T(2,128)}) fusion(f32[2,1770240]{1,0:T(2,128)} %constant_dynamic-update-slice_fusion, s32[2]{0:T(128)S(1)} %copy-done.37), kind=kOutput, calls=%fused_computation.55 | convolution fusion | flops 92052480 | bytes 28323856 | tf_op jit(solution)/shard_map/dot_general | solution.py:316
  1043.8 6.4 psum.14
  1050.1 119.3 %convolution_reduce_fusion = f32[1770240]{0:T(1024)} fusion(f32[2,1770240]{1,0:T(2,128)} %get-tuple-element.263, f32[2]{0:T(128)S(1)} %sqrt.7), kind=kOutput, calls=%fused_computation.116 | convolution fusion | flops 42485764 | bytes 21242888 | tf_op jit(solution)/shard_map/dot_general | solution.py:320
  1169.4 65.6 %scatter_custom_fusion = s32[20752]{0:T(1024)S(1)} fusion(s32[13830]{0:T(1024)} %copy-done.27, s32[13830]{0:T(1024)S(1)} %iota.92, s32[]{:T(128)} %constant.72.clone.1), kind=kCustom, calls=%fused_computation.158 | custom fusion | bytes 83520 | tf_op jit(solution)/shard_map/scatter | solution.py:326
  1246.7 157.5 %all-reduce.2.cloned.1.call-done = f32[13830,128]{1,0:T(8,128)} async-done(((f32[13830,128]{1,0:T(8,128)}), f32[13830,128]{1,0:T(8,128)}) %all-reduce.2.cloned.1.call-update) | async-done | bytes 7080976 | tf_op jit(solution)/shard_map/psum | solution.py:329
  1404.2 7.7 gather_fusion.1
  1417.1 9.0 copy.86
  1426.1 9.0 copy.88
  1435.1 9.0 copy.87
  (270 shorter events, 193.2 us)
Async XLA Ops:
  7.2 7.7 copy-start.35
  7.2 158.7 %all-gather.10.cloned.1.call-start = ((), (), s32[]{:S(2)}) async-start(), calls=%async_computation.10 | async-start | bytes 11953152 | tf_op jit(solution)/shard_map/all_gather | solution.py:141
  10.8 217.5 %all-gather.6.cloned.1.call-start = ((), (), s32[]{:S(2)}) async-start(), calls=%async_computation.4 | async-start | bytes 7864320 | tf_op jit(solution)/shard_map/all_gather | solution.py:147
  11.6 248.4 %all-gather.8.cloned.1.call-start = ((), (), s32[]{:S(2)}) async-start(), calls=%async_computation.6 | async-start | bytes 7864320 | tf_op jit(solution)/shard_map/all_gather | solution.py:204
  12.3 929.1 %reduce-scatter.9.cloned.1.call-start = ((), (), s32[]{:S(2)}) async-start(), calls=%async_computation.7 | async-start | bytes 7864320 | tf_op jit(solution)/shard_map/reduce_scatter | solution.py:269
  214.3 20.6 %copy-start.31 = (f32[768]{0:T(1024)}, f32[768]{0:T(1024)S(1)}, u32[]{:S(2)}) copy-start(f32[768]{0:T(1024)S(1)} %mul.459) | copy-start | bytes 9220
  214.4 20.5 %copy-start.33 = (f32[768]{0:T(1024)}, f32[768]{0:T(1024)S(1)}, u32[]{:S(2)}) copy-start(f32[768]{0:T(1024)S(1)} %mul.475) | copy-start | bytes 9220
  220.0 6.4 copy-start.16
  225.8 6.4 copy-start.17
  228.3 4.7 copy-start.3
  232.2 2.7 copy-start.36
  234.9 7.9 copy-start.30
  242.8 3.9 copy-start.12
  246.9 13.1 copy-start.18
  269.5 3.6 copy-start.11
  269.5 3.8 copy-start.23
  269.5 3.8 copy-start.25
  273.3 2.8 copy-start.29
  273.3 2.8 copy-start.39
  292.1 12.1 copy-start.7
  332.9 12.1 copy-start.7
  373.7 12.1 copy-start.7
  414.5 12.1 copy-start.7
  439.5 3.3 copy-start.1
  502.9 4.5 copy-start
  512.5 9.5 copy-start.2
  522.0 3.3 copy-start.1
  586.3 4.5 copy-start
  596.9 9.5 copy-start.2
  606.4 3.3 copy-start.1
  670.7 4.5 copy-start
  681.3 9.5 copy-start.2
  690.9 3.3 copy-start.1
  755.1 4.5 copy-start
  765.7 9.5 copy-start.2
  775.6 4.1 copy-start.24
  775.6 4.1 copy-start.26
  788.4 9.5 copy-start.9
  799.1 9.3 slice-start
  801.7 6.7 slice-start.1
  806.5 7.2 slice-start.4
  808.4 5.2 slice-start.5
  838.3 129.8 %reduce-scatter.11.cloned.1.call-start = ((), (), s32[]{:S(2)}) async-start(), calls=%async_computation.8 | async-start | bytes 7864320 | tf_op jit(solution)/shard_map/reduce_scatter | solution.py:272
  838.3 35.7 %slice-start.2 = ((s8[6291456]{0:T(1024)(128)(4,1)}), s8[4194304]{0:T(1024)(128)(4,1)S(1)}, s32[]{:S(2)}) async-start(s8[6291456]{0:T(1024)(128)(4,1)} %bitcast.218), calls=%async_computation.14 | async-start | bytes 8388608
  840.6 33.3 %slice-start.3 = ((s8[6291456]{0:T(1024)(128)(4,1)}), s8[2097152]{0:T(1024)(128)(4,1)S(1)}, s32[]{:S(2)}) async-start(s8[6291456]{0:T(1024)(128)(4,1)} %bitcast.218), calls=%async_computation.15 | async-start | bytes 4194304
  840.7 33.3 %copy-start.20 = (bf16[768,768]{1,0:T(8,128)(2,1)S(1)}, bf16[768,768]{1,0:T(8,128)(2,1)}, u32[]{:S(2)}) copy-start(bf16[768,768]{1,0:T(8,128)(2,1)} %reshape.377) | copy-start | bytes 3538948
  883.2 2.6 copy-start.38
  902.2 5.8 copy-start.15
  909.1 91.2 %reduce-scatter.13.cloned.1.call-start = ((), (), s32[]{:S(2)}) async-start(), calls=%async_computation.11 | async-start | bytes 491520
  909.1 6.2 copy-start.10
  917.7 12.2 copy-start.21
  929.9 11.5 copy-start.28
  946.8 30.2 %copy-start.19 = (bf16[192,768]{1,0:T(8,128)(2,1)S(1)}, bf16[192,768]{1,0:T(8,128)(2,1)}, u32[]{:S(2)}) copy-start(bf16[192,768]{1,0:T(8,128)(2,1)} %reshape.375) | copy-start | bytes 884740
  968.1 3.8 copy-start.6
  976.5 262.1 %reduce-scatter.7.cloned.1.call-start = ((), (), s32[]{:S(2)}) async-start(), calls=%async_computation.5 | async-start | bytes 7864320 | tf_op jit(solution)/shard_map/reduce_scatter | solution.py:200
  994.2 410.0 %all-reduce.2.cloned.1.call-start = ((), (), s32[]{:S(2)}) async-start(), calls=%async_computation.9 | async-start | bytes 14163968 | tf_op jit(solution)/shard_map/psum | solution.py:329
  994.3 8.0 copy-start.37
  1050.1 119.3 %copy-start.40 = (f32[2]{0:T(128)}, f32[2]{0:T(128)S(1)}, u32[]{:S(2)}) copy-start(f32[2]{0:T(128)S(1)} %sqrt.7) | copy-start | bytes 28
  1169.4 65.9 %copy-start.5 = (bf16[1024,768]{1,0:T(8,128)(2,1)S(1)}, bf16[1024,768]{1,0:T(8,128)(2,1)}, u32[]{:S(2)}) copy-start(bf16[1024,768]{1,0:T(8,128)(2,1)} %reduce-scatter.9.cloned.1.call-done) | copy-start | bytes 4718596
  1169.4 65.9 %copy-start.32 = (f32[768]{0:T(1024)S(1)}, f32[768]{0:T(1024)}, u32[]{:S(2)}) copy-start(f32[768]{0:T(1024)} %copy-done.31) | copy-start | bytes 9220
  1169.4 65.9 %copy-start.34 = (f32[768]{0:T(1024)S(1)}, f32[768]{0:T(1024)}, u32[]{:S(2)}) copy-start(f32[768]{0:T(1024)} %copy-done.33) | copy-start | bytes 9220
  1235.3 7.0 dynamic-slice-start
  1238.6 3.6 copy-start.13
  1246.7 165.3 %copy-start.14 = (f32[1,2594,128]{2,0,1:T(1,128)S(1)}, f32[1,2594,128]{2,0,1:T(1,128)}, u32[]{:S(2)}) copy-start(f32[1,2594,128]{2,0,1:T(1,128)} %param.15) | copy-start | bytes 3984388
  (7 other events, 9.8 us)
Sparse Core Ops, SparseCore 0:
  10.9 154.8 all-gather.9
  167.4 44.5 all-gather.5
  213.6 46.4 all-gather.7
  838.4 58.8 reduce-scatter.8
  909.2 58.8 reduce-scatter.10
  976.7 20.7 reduce-scatter.12
  1000.0 58.9 reduce-scatter.6
  1169.5 234.6 all-reduce.1
where the time goes:
time: 1460 us; the launch traced here: 1450 us
  matrix products  624 us (43%)
  waiting for transfers between devices  339 us (23%)
  local copies, waits for them, and re-layouts  273 us (19%)
  other arithmetic  172 us (12%)
  loops' own time  16.5 us (1%)
  between operations  15.2 us (1%)
    psum x1, waiting for transfers between devices, on_device(): summed = lax.psum(grad_rows, 'dp')  158 us
    all_gather x1, waiting for transfers between devices, on_device(): lax.all_gather(master[0].astype(jnp.bfloat16), 'dp', axis=0, tiled=True)  149 us
    dot_general x1, matrix products, on_device(): clipped = jnp.dot(clip_scale, group_grads, precision=lax.Precision.HIGHEST)  119 us
    dot_general x8, matrix products, scores_of(): jnp.einsum('sqhd,skhd->shqk', query_block, key_rows, preferred_element_ty...  93.7 us
    unnamed x100, local copies, waits for them, and re-layouts  83.8 us
    dot_general x4, matrix products, backward_block(): jnp.einsum('sqhd,skhd->shqk', grad_block, values, preferred_element_type=...  72.5 us
    convert_element_type x4, other arithmetic, backward_block(): grad_scores = (probs * (grad_probs - row_dot)).astype(jnp.bfloat16)  68.2 us
    scatter x1, local copies, waits for them, and re-layouts, on_device(): slot_block = jnp.full((slot_total,), -1, jnp.int32).at[block_slot].set(jn...  65.6 us
  transfers between devices with their start and end apart: 8, of which 4 were waited for; matrix products, arithmetic and copies ran while one was open for 31% of the time, Pallas kernels for 0%

commit v1 on v0

--- a/solution.py
+++ b/solution.py
@@ -326,7 +326,9 @@
         .set(jnp.arange(block_count, dtype=jnp.int32))
     )
     my_blocks = lax.dynamic_slice_in_dim(slot_block, owner_index * capacity, capacity)
-    summed = lax.psum(grad_rows, "dp")
+    summed = grad_rows
+    for hop in (1, 2, 4):
+        summed = summed + lax.ppermute(summed, "dp", [(dev, dev ^ hop) for dev in range(8)])
     owned_grad = jnp.where(my_blocks[:, None] >= 0, summed[jnp.maximum(my_blocks, 0)], 0.0)
     position = (
         jnp.maximum(my_blocks, 0)[:, None] * block_width

time: 1460 us -> 1840 us (1.26)
  waiting for transfers between devices: 339 us -> 721 us
  matrix products: 624 us -> 597 us
  other arithmetic: 172 us -> 194 us
    ppermute x0 -> x3, waiting for transfers between devices: none -> 513 us  [on_device(): lax.ppermute(summed, 'dp', [(dev, dev ^ hop) for dev in range(8)])]
    psum x1 -> x0, waiting for transfers between devices: 158 us -> none  [on_device(): summed = lax.psum(grad_rows, 'dp')]
    add x0 -> x3, other arithmetic: none -> 22.8 us  [on_device(): summed + lax.ppermute(summed, 'dp', [(dev, dev ^ hop) for dev in range(8)])]
    unnamed x100 -> x106, local copies, waits for them, and re-layouts: 83.8 us -> 81.6 us
  transfers between devices with their start and end apart: 8 -> 10, of which waited for: 4 -> 7; matrix products, arithmetic and copies ran while one was open for 31% -> 16% of each run, Pallas kernels for 0% -> 0%
where the time goes in v1:
time: 1840 us; the launch traced here: 1830 us
  waiting for transfers between devices  721 us (39%)
  matrix products  597 us (32%)
  local copies, waits for them, and re-layouts  273 us (15%)
  other arithmetic  194 us (11%)
    ppermute x3, waiting for transfers between devices, on_device(): lax.ppermute(summed, 'dp', [(dev, dev ^ hop) for dev in range(8)])  513 us
    all_gather x1, waiting for transfers between devices, on_device(): lax.all_gather(master[0].astype(jnp.bfloat16), 'dp', axis=0, tiled=True)  149 us
    dot_general x1, matrix products, on_device(): clipped = jnp.dot(clip_scale, group_grads, precision=lax.Precision.HIGHEST)  104 us
    dot_general x8, matrix products, scores_of(): jnp.einsum('sqhd,skhd->shqk', query_block, key_rows, preferred_element_ty...  93.8 us
    unnamed x106, local copies, waits for them, and re-layouts  81.6 us
    dot_general x4, matrix products, backward_block(): jnp.einsum('sqhd,skhd->shqk', grad_block, values, preferred_element_type=...  72.6 us
    convert_element_type x4, other arithmetic, backward_block(): grad_scores = (probs * (grad_probs - row_dot)).astype(jnp.bfloat16)  68.2 us
    scatter x1, local copies, waits for them, and re-layouts, on_device(): slot_block = jnp.full((slot_total,), -1, jnp.int32).at[block_slot].set(jn...  65.5 us
  transfers between devices with their start and end apart: 10, of which 7 were waited for; matrix products, arithmetic and copies ran while one was open for 16% of the time, Pallas kernels for 0%

profile of v1, /device:TPU:0, one launch (start us, length us, event | category | flops | bytes accessed | tf_op | source)
XLA Modules:
  0.0 1832.6 jit_solution(11544767130036350931)
XLA Ops:
  17.1 148.7 %all-gather.10.cloned.1.call-done = bf16[1,20752,128]{2,0,1:T(2,128)(2,1)} async-done(((bf16[1,2594,128]{2,0,1:T(2,128)(2,1)}), bf16[1,20752,128]{2,0,1:T(2,128)(2,1)}) %all-gather.10.cloned.1.call-update) | async-done | bytes 5312528 | tf_op jit(solution)/shard_map/all_gather | solution.py:141
  165.9 8.5 copy.115
  174.4 30.7 %gather_fusion = bf16[13830,128]{1,0:T(8,128)(2,1)S(1)} fusion(bf16[20752,128]{1,0:T(8,128)(2,1)} %bitcast.206, s32[14336]{0:T(1024)} %pad_clamp_fusion), kind=kCustom, calls=%fused_computation | custom fusion | bytes 7136280 | tf_op jit(solution)/shard_map/gather | solution.py:142
  234.8 7.9 fusion.36
  249.9 10.1 all-gather.8.cloned.1.call-done
  276.0 163.2 %while.30 = (s32[]{:T(128)}, bf16[4,2,512,3,64]{2,4,3,1,0:T(8,128)(2,1)}, f32[4,2,3,512,1]{3,2,1,4,0:T(4,128)S(1)}, s32[4]{0:T(128)S(1)}, bf16[2,2048,3,64]{1,3,...) while((s32[]{:T(128)}, ...), condition=%wide.region_5.6_spmd.clone.clone, body=%wide.region_2.5_spmd.clone.sunk.clone | while | flops 1687156224 | bytes 96723152 | solution.py:193
  279.9 12.1 fusion.179
  292.0 12.1 fusion.180
  304.1 11.6 fusion.181
  320.7 12.1 fusion.179
  332.8 12.1 fusion.180
  344.9 11.6 fusion.181
  361.5 12.1 fusion.179
  373.6 12.1 fusion.180
  385.7 11.6 fusion.181
  402.3 12.1 fusion.179
  414.4 12.1 fusion.180
  426.5 11.6 fusion.181
  439.2 336.3 %while.31 = (s32[]{:T(128)}, f32[2,2048,3,64]{1,3,2,0:T(8,128)}, f32[2,2048,3,64]{1,3,2,0:T(8,128)}, f32[4,2,512,3,64]{2,4,3,1,0:T(8,128)}, s32[4]{0:T(128)S(1)}...) while((s32[]{:T(128)}, f32[2,2048,3,64]{1,3,2,0:T(8,128)}, ...), condition=%wide.region_9.10_spmd.clone.clone, body=%wide.region_7.9_spmd.clone.sunk.clone | while | flops 4126078464 | bytes 275603712 | solution.py:249
  443.4 11.3 fusion.191
  454.7 12.9 bitcast_add_fusion.8
  467.6 18.1 multiply_reduce_fusion.4
  485.8 17.0 multiply_convert_fusion.3
  512.4 9.5 fusion.192
  525.9 11.3 fusion.191
  537.2 13.8 bitcast_add_fusion.8
  551.0 18.1 multiply_reduce_fusion.4
  569.1 17.0 multiply_convert_fusion.3
  590.7 6.1 bitcast_add_fusion.7
  596.8 9.5 fusion.192
  610.3 11.3 fusion.191
  621.6 13.8 bitcast_add_fusion.8
  635.4 18.1 multiply_reduce_fusion.4
  653.6 17.0 multiply_convert_fusion.3
  681.2 9.5 fusion.192
  694.7 11.3 fusion.191
  706.0 13.8 bitcast_add_fusion.8
  719.8 18.1 multiply_reduce_fusion.4
  737.9 17.0 multiply_convert_fusion.3
  765.6 9.5 fusion.192
  788.3 9.6 copy.74
  813.6 9.8 fusion.108
  828.8 9.3 convolution_convert_fusion
  840.6 33.3 %fusion.41 = (bf16[4096,768]{1,0:T(8,128)(2,1)}, f32[4096,768]{1,0:T(8,128)S(1)}) fusion(bf16[4096,768]{1,0:T(8,128)(2,1)} %get-tuple-element.243, bf16[768,768]{1,0:T(8,128)(2,1)S(1)} %copy-done.23), kind=kOutput, calls=%fused_computation.59 | convolution fusion | flops 5036310528 | bytes 26345472 | tf_op jit(solution)/shard_map/dot_general | solution.py:195
  874.0 9.2 fusion.47
  885.7 7.1 convolution_convert_fusion.1
  892.9 9.2 convolution_bitcast_fusion.1
  909.0 7.3 constant_dynamic-update-slice_fusion.2
  916.2 8.0 convolution_bitcast_fusion
  935.8 32.1 %reduce-scatter.11.cloned.1.call-done = bf16[1024,768]{1,0:T(8,128)(2,1)} async-done(((bf16[4096,768]{1,0:T(8,128)(2,1)}), bf16[1024,768]{1,0:T(8,128)(2,1)}) %reduce-scatter.11.cloned.1.call-update) | async-done | bytes 1572880 | tf_op jit(solution)/shard_map/reduce_scatter | solution.py:272
  980.2 14.9 reduce-scatter.13.cloned.1.call-done
  997.1 41.5 %multiply_reduce_fusion.1 = (f32[2]{0:T(128)S(1)}, f32[2,1770240]{1,0:T(2,128)}) fusion(f32[2,1770240]{1,0:T(2,128)} %constant_dynamic-update-slice_fusion, s32[2]{0:T(128)S(1)} %copy-done.38), kind=kOutput, calls=%fused_computation.55 | convolution fusion | flops 92052480 | bytes 28323856 | tf_op jit(solution)/shard_map/dot_general | solution.py:316
  1044.4 103.7 %convolution_reduce_fusion = f32[1770240]{0:T(1024)S(1)} fusion(f32[2,1770240]{1,0:T(2,128)} %get-tuple-element.263, f32[2]{0:T(128)S(1)} %sqrt.7), kind=kOutput, calls=%fused_computation.116 | convolution fusion | flops 42485764 | bytes 21242888 | tf_op jit(solution)/shard_map/dot_general | solution.py:320
  1149.8 152.5 %collective-permute-done = f32[13830,128]{1,0:T(8,128)S(1)} collective-permute-done((f32[13830,128]{1,0:T(8,128)S(1)}, f32[13830,128]{1,0:T(8,128)S(1)}, u32[]{:S(2)}, u32[]{:S(2)}) %collective-permute-start) | collective-permute-done | bytes 7080992 | tf_op jit(solution)/shard_map/ppermute | solution.py:331
  1314.0 7.7 fusion.107
  1326.3 134.6 %collective-permute-done.1 = f32[13830,128]{1,0:T(8,128)} collective-permute-done((f32[13830,128]{1,0:T(8,128)}, f32[13830,128]{1,0:T(8,128)}, u32[]{:S(2)}, u32[]{:S(2)}) %collective-permute-start.1) | collective-permute-done | bytes 7080992 | tf_op jit(solution)/shard_map/ppermute | solution.py:331
  1460.9 10.7 fusion.144
  1473.8 65.5 %scatter_custom_fusion = s32[20752]{0:T(1024)S(1)} fusion(s32[13830]{0:T(1024)} %copy-done.28, s32[13830]{0:T(1024)S(1)} %iota.92, s32[]{:T(128)} %constant.72.clone.1), kind=kCustom, calls=%fused_computation.158 | custom fusion | bytes 83520 | tf_op jit(solution)/shard_map/scatter | solution.py:326
  1550.9 226.1 %collective-permute-done.2 = f32[13830,128]{1,0:T(8,128)} collective-permute-done((f32[13830,128]{1,0:T(8,128)}, f32[13830,128]{1,0:T(8,128)}, u32[]{:S(2)}, u32[]{:S(2)}) %collective-permute-start.2) | collective-permute-done | bytes 7080992 | tf_op jit(solution)/shard_map/ppermute | solution.py:331
  1777.0 8.5 add.239
  1785.5 7.8 gather_fusion.1
  1798.6 9.0 copy.86
  1807.6 9.0 copy.88
  1816.5 9.0 copy.87
  (283 shorter events, 232.2 us)
Async XLA Ops:
  7.2 7.7 copy-start.36
  7.2 158.7 %all-gather.10.cloned.1.call-start = ((), (), s32[]{:S(2)}) async-start(), calls=%async_computation.9 | async-start | bytes 11953152 | tf_op jit(solution)/shard_map/all_gather | solution.py:141
  10.8 217.4 %all-gather.6.cloned.1.call-start = ((), (), s32[]{:S(2)}) async-start(), calls=%async_computation.4 | async-start | bytes 7864320 | tf_op jit(solution)/shard_map/all_gather | solution.py:147
  11.6 248.4 %all-gather.8.cloned.1.call-start = ((), (), s32[]{:S(2)}) async-start(), calls=%async_computation.6 | async-start | bytes 7864320 | tf_op jit(solution)/shard_map/all_gather | solution.py:204
  12.3 917.7 %reduce-scatter.9.cloned.1.call-start = ((), (), s32[]{:S(2)}) async-start(), calls=%async_computation.7 | async-start | bytes 7864320 | tf_op jit(solution)/shard_map/reduce_scatter | solution.py:269
  214.3 20.5 %copy-start.32 = (f32[768]{0:T(1024)}, f32[768]{0:T(1024)S(1)}, u32[]{:S(2)}) copy-start(f32[768]{0:T(1024)S(1)} %mul.459) | copy-start | bytes 9220
  214.4 20.4 %copy-start.34 = (f32[768]{0:T(1024)}, f32[768]{0:T(1024)S(1)}, u32[]{:S(2)}) copy-start(f32[768]{0:T(1024)S(1)} %mul.475) | copy-start | bytes 9220
  220.0 6.4 copy-start.18
  225.7 6.4 copy-start.19
  228.2 4.7 copy-start.3
  234.8 7.9 copy-start.31
  242.7 3.9 copy-start.14
  246.8 13.2 copy-start.20
  269.4 3.6 copy-start.13
  269.5 3.8 copy-start.24
  269.5 3.8 copy-start.26
  292.0 12.1 copy-start.9
  332.8 12.1 copy-start.9
  373.6 12.1 copy-start.9
  414.4 12.1 copy-start.9
  439.4 3.3 copy-start.1
  502.8 4.5 copy-start
  512.4 9.5 copy-start.2
  521.9 3.3 copy-start.1
  586.2 4.5 copy-start
  596.8 9.5 copy-start.2
  606.4 3.3 copy-start.1
  670.6 4.5 copy-start
  681.2 9.5 copy-start.2
  755.0 4.5 copy-start
  765.6 9.5 copy-start.2
  775.5 4.1 copy-start.25
  775.5 4.1 copy-start.27
  788.3 9.6 copy-start.11
  799.1 9.3 slice-start
  801.6 6.8 slice-start.1
  806.4 7.1 slice-start.6
  808.4 5.2 slice-start.7
  838.2 129.7 %reduce-scatter.11.cloned.1.call-start = ((), (), s32[]{:S(2)}) async-start(), calls=%async_computation.8 | async-start | bytes 7864320 | tf_op jit(solution)/shard_map/reduce_scatter | solution.py:272
  838.3 35.7 %slice-start.2 = ((s8[6291456]{0:T(1024)(128)(4,1)}), s8[4194304]{0:T(1024)(128)(4,1)S(1)}, s32[]{:S(2)}) async-start(s8[6291456]{0:T(1024)(128)(4,1)} %bitcast.220), calls=%async_computation.13 | async-start | bytes 8388608
  840.6 33.4 %slice-start.3 = ((s8[6291456]{0:T(1024)(128)(4,1)}), s8[2097152]{0:T(1024)(128)(4,1)S(1)}, s32[]{:S(2)}) async-start(s8[6291456]{0:T(1024)(128)(4,1)} %bitcast.220), calls=%async_computation.14 | async-start | bytes 4194304
  840.6 33.4 %copy-start.22 = (bf16[768,768]{1,0:T(8,128)(2,1)S(1)}, bf16[768,768]{1,0:T(8,128)(2,1)}, u32[]{:S(2)}) copy-start(bf16[768,768]{1,0:T(8,128)(2,1)} %reshape.377) | copy-start | bytes 3538948
  902.1 5.8 copy-start.17
  908.9 7.3 slice-start.4
  908.9 86.2 %reduce-scatter.13.cloned.1.call-start = ((), (), s32[]{:S(2)}) async-start(), calls=%async_computation.10 | async-start | bytes 491520
  909.0 7.3 slice-start.5
  924.2 5.8 copy-start.29
  967.9 3.8 copy-start.8
  974.2 568.6 %reduce-scatter.7.cloned.1.call-start = ((), (), s32[]{:S(2)}) async-start(), calls=%async_computation.5 | async-start | bytes 7864320 | tf_op jit(solution)/shard_map/reduce_scatter | solution.py:200
  974.2 22.9 %copy-start.38 = (s32[2]{0:T(128)S(1)}, s32[2]{0:T(128)}, u32[]{:S(2)}) copy-start(s32[2]{0:T(128)} %param.13) | copy-start | bytes 28
  1044.4 103.7 %copy-start.41 = (f32[2]{0:T(128)}, f32[2]{0:T(128)S(1)}, u32[]{:S(2)}) copy-start(f32[2]{0:T(128)S(1)} %sqrt.7) | copy-start | bytes 28
  1148.1 157.8 %copy-start.5 = (f32[1770240]{0:T(1024)}, f32[1770240]{0:T(1024)S(1)}, u32[]{:S(2)}) copy-start(f32[1770240]{0:T(1024)S(1)} %convolution_reduce_fusion) | copy-start | bytes 21242884
  1148.1 160.7 %copy-start.12 = (bf16[4,2,512,3,64]{2,4,3,1,0:T(8,128)(2,1)S(1)}, bf16[4,2,512,3,64]{2,4,3,1,0:T(8,128)(2,1)}, u32[]{:S(2)}) copy-start(bf16[4,2,512,3,64]{2,4,3,1,0:T(8,128)(2,1)} %get-tuple-element.108) | copy-start | bytes 4718596
  1148.1 154.2 %collective-permute-start = (f32[13830,128]{1,0:T(8,128)S(1)}, f32[13830,128]{1,0:T(8,128)S(1)}, u32[]{:S(2)}, u32[]{:S(2)}) collective-permute-start(f32[13830,128]{1,0:T(8,128)S(1)} %bitcast.207), channel_id=1, source_target_pairs={{0,4},{4,0},{8,12},{12,8},{16,20},{20,16},{24,28},{28,24},{1,5},{5... | collective-permute-start | bytes 21242888 | tf_op jit(solution)/shard_map/ppermute | solution.py:331
  1302.3 5.0 copy-start.6
  1307.3 153.6 %collective-permute-start.1 = (f32[13830,128]{1,0:T(8,128)}, f32[13830,128]{1,0:T(8,128)}, u32[]{:S(2)}, u32[]{:S(2)}) collective-permute-start(f32[13830,128]{1,0:T(8,128)} %bitcast_add_fusion.2), channel_id=1, source_target_pairs={{0,8},{4,12},{8,0},{12,4},{16,24},{20,28},{24,16},{28,20},{1,9},{5... | collective-permute-start | bytes 21242888 | tf_op jit(solution)/shard_map/ppermute | solution.py:331
  1314.0 7.7 copy-start.21
  1326.3 213.2 %copy-start.7 = (bf16[1024,768]{1,0:T(8,128)(2,1)S(1)}, bf16[1024,768]{1,0:T(8,128)(2,1)}, u32[]{:S(2)}) copy-start(bf16[1024,768]{1,0:T(8,128)(2,1)} %reduce-scatter.9.cloned.1.call-done) | copy-start | bytes 4718596
  1326.3 213.2 %copy-start.33 = (f32[768]{0:T(1024)S(1)}, f32[768]{0:T(1024)}, u32[]{:S(2)}) copy-start(f32[768]{0:T(1024)} %copy-done.32) | copy-start | bytes 9220
  1326.3 213.2 %copy-start.35 = (f32[768]{0:T(1024)S(1)}, f32[768]{0:T(1024)}, u32[]{:S(2)}) copy-start(f32[768]{0:T(1024)} %copy-done.34) | copy-start | bytes 9220
  1471.6 305.4 %collective-permute-start.2 = (f32[13830,128]{1,0:T(8,128)}, f32[13830,128]{1,0:T(8,128)}, u32[]{:S(2)}, u32[]{:S(2)}) collective-permute-start(f32[13830,128]{1,0:T(8,128)} %fusion.144), channel_id=1, source_target_pairs={{0,16},{4,20},{8,24},{12,28},{16,0},{20,4},{24,8},{28,12},{1,17},{... | collective-permute-start | bytes 21242888 | tf_op jit(solution)/shard_map/ppermute | solution.py:331
  1539.5 6.8 dynamic-slice-start
  1542.8 3.5 copy-start.15
  1785.5 7.9 copy-start.16
  (12 other events, 23.9 us)
Sparse Core Ops, SparseCore 0:
  10.9 154.8 all-gather.9
  167.4 44.5 all-gather.5
  213.6 46.4 all-gather.7
  838.3 58.8 reduce-scatter.8
  909.0 58.8 reduce-scatter.10
  974.3 20.7 reduce-scatter.12
  1326.4 57.9 reduce-scatter.6
